TPU v7x, 32 devices: a whole 2x2x4 slice. The times are simulated.
32 devices in a mesh: geom: 2 (over x), row: 8 (over z, y), col: 2 (over core).
Axes of the slice: x: 2, y: 2, z: 4, core: 2. Of those that a mesh axis runs over, the one named last changes fastest.
Arguments:
- matrix: bfloat16 [128, 8, 128, 128], P(('geom', 'row'), 'col'), parts along dimension 0, may hold values from -1.5 to 1.5
- columns: int32 [64, 8], P('row'), may hold values from -1 to 63, as said below
Outputs:
- purified: bfloat16 [128, 8, 128, 128], P(('geom', 'row'), 'col'), parts along dimension 0
There are 2 independent parts, one for each index of `geom`. A program takes and returns all parts, laid end to end along the dimension named above; an argument that names none is the same for every part. Nothing has to cross between parts.
Inputs may be any that keep to these rules, and one draw needn't show every extreme that they name: In block row i the valid slots come first and slot 0 holds i; valid slots hold distinct columns (i + d) mod 64 with -4 <= d <= 4, and the others hold -1. A block row has 1 to 8 valid slots, and some block row has 8.
All inputs are finite; a program needn't handle non-finite values.
Results may differ from a plain program's by a relative error of at most 0.0049.
Values may be sent and summed in bfloat16 or wider, within the bound.
A program may use at most 64 MiB of HBM per device.

v0:
```python
import jax
import jax.numpy as jnp
from jax import lax
from jax.sharding import PartitionSpec as P

REACH = 4


group_rows = 8


def from_behind(value, axis, by):
    devices = lax.axis_size(axis)
    return lax.ppermute(value, axis, [(i, (i + by) % devices) for i in range(devices)])


def local(matrix, columns):
    local_rows = matrix.shape[0]
    own_slots = matrix.shape[1]
    block_size = matrix.shape[2]
    slot_count = columns.shape[1]
    reach_rows = REACH
    total_rows = local_rows * lax.axis_size("row")
    row_start = lax.axis_index("row") * local_rows
    first_slot = lax.axis_index("col") * own_slots
    whole_rows = lax.all_gather(matrix, "col", axis=1, tiled=True)
    from_below = from_behind(
        (whole_rows[local_rows - reach_rows :], columns[local_rows - reach_rows :]), "row", 1
    )
    from_above = from_behind((whole_rows[:reach_rows], columns[:reach_rows]), "row", -1)
    panel_rows = jnp.concatenate([from_below[0], whole_rows, from_above[0]], axis=0)
    panel_cols = jnp.concatenate([from_below[1], columns, from_above[1]], axis=0)
    own_targets = lax.dynamic_slice_in_dim(columns, first_slot, own_slots, 1)
    slot_ids = jnp.arange(slot_count, dtype=jnp.int32)
    empty_index = panel_rows.shape[0] * slot_count
    flat_blocks = jnp.concatenate(
        [
            panel_rows.reshape(-1, block_size, block_size),
            jnp.zeros((1, block_size, block_size), panel_rows.dtype),
        ],
        axis=0,
    )

    def partial_product(left_blocks, index_table):
        left_slots = left_blocks.shape[1]
        out_slots = index_table.shape[2]
        groups = local_rows // group_rows

        def one_group(inputs):
            left_group, index_group = inputs
            picked = flat_blocks[index_group]
            return jnp.einsum(
                "ijab,ijsbc->isac", left_group, picked, preferred_element_type=jnp.float32
            )

        stacked = lax.map(
            one_group,
            (
                left_blocks.reshape(groups, group_rows, left_slots, block_size, block_size),
                index_table.reshape(groups, group_rows, left_slots, out_slots),
            ),
        )
        return stacked.reshape(local_rows, out_slots, block_size, block_size)

    has_source = columns >= 0
    position = jnp.where(has_source, (columns - row_start + reach_rows) % total_rows, 0)
    source_cols = panel_cols[position]
    matches = (
        (source_cols[:, :, None, :] == own_targets[:, None, :, None])
        & (own_targets[:, None, :, None] >= 0)
        & has_source[:, :, None, None]
    )
    chosen = jnp.sum(jnp.where(matches, slot_ids, 0), axis=3)
    found_match = jnp.any(matches, axis=3)
    index_table = jnp.where(found_match, position[:, :, None] * slot_count + chosen, empty_index)
    live_count = jnp.sum(has_source.astype(jnp.int32), axis=1)
    index_table, live_count = (index_table, live_count)
    square = partial_product(whole_rows, index_table).astype(jnp.bfloat16)
    square_whole = lax.all_gather(square, "col", axis=1, tiled=True)
    cube_sum = partial_product(square_whole, index_table)
    return (3.0 * square.astype(jnp.float32) - 2.0 * cube_sum).astype(jnp.bfloat16)


def solution(mesh):
    placed = (P(("geom", "row"), "col", None, None), P("row", None))
    return jax.shard_map(
        local,
        mesh=mesh,
        in_specs=placed,
        out_specs=P(("geom", "row"), "col", None, None),
        check_vma=False,
    )
```

profile of v0, /device:TPU:0, one launch (start us, length us, event | category | flops | bytes accessed | tf_op | source)
XLA Modules:
  0.0 122.7 jit_solution(10887109171620727217)
XLA Ops:
  6.5 0.0 all-gather.3.cloned.1.call-start
  6.5 0.7 all-gather.3.cloned.1.call-update
  7.3 0.0 all-gather.5.cloned.1.call-start
  7.3 0.8 fusion.19
  8.1 3.0 %collective-permute-start.2 = (s32[4,8]{1,0:T(4,128)S(1)}, s32[4,8]{1,0:T(4,128)S(1)}, u32[]{:S(2)}, u32[]{:S(2)}) collective-permute-start(s32[4,8]{1,0:T(4,128)S(1)} %get-tuple-element.34), channel_id=1, source_target_pairs={{0,2},{2,4},{4,6},{6,8},{8,10},{10,12},{12,14},{14,0},{1,3},{3,5},... | collective-permute-start | bytes 392 | tf_op jit(solution)/shard_map/ppermute | solution.py:14
  11.1 3.0 %collective-permute-start.3 = (s32[4,8]{1,0:T(4,128)S(1)}, s32[4,8]{1,0:T(4,128)S(1)}, u32[]{:S(2)}, u32[]{:S(2)}) collective-permute-start(s32[4,8]{1,0:T(4,128)S(1)} %get-tuple-element.40), channel_id=1, source_target_pairs={{0,14},{2,0},{4,2},{6,4},{8,6},{10,8},{12,10},{14,12},{1,15},{3,1}... | collective-permute-start | bytes 392 | tf_op jit(solution)/shard_map/ppermute | solution.py:14
  14.1 0.7 broadcast_multiply_fusion
  14.8 7.4 %all-gather.3.cloned.1.call-done = bf16[8,8,128,128]{3,2,1,0:T(8,128)(2,1)} async-done(((bf16[8,4,128,128]{3,2,1,0:T(8,128)(2,1)}), bf16[8,8,128,128]{3,2,1,0:T(8,128)(2,1)}) %all-gather.3.cloned.1.call-update) | async-done | bytes 2097168 | tf_op jit(solution)/shard_map/all_gather | solution.py:26
  22.2 2.9 %fusion.18 = (bf16[4,8,128,128]{3,2,1,0:T(8,128)(2,1)}, bf16[4,8,128,128]{3,2,1,0:T(8,128)(2,1)S(1)}) fusion(bf16[8,8,128,128]{3,2,1,0:T(8,128)(2,1)} %all-gather.3.cloned.1.call-done), kind=kLoop, calls=%fused_computation.32 | loop fusion | bytes 4194304 | tf_op jit(solution)/shard_map/slice | solution.py:28
  25.1 1.7 %collective-permute-start = (bf16[4,8,128,128]{3,2,1,0:T(8,128)(2,1)}, bf16[4,8,128,128]{3,2,1,0:T(8,128)(2,1)}, u32[]{:S(2)}, u32[]{:S(2)}) collective-permute-start(bf16[4,8,128,128]{3,2,1,0:T(8,128)(2,1)} %get-tuple-element.30), channel_id=1, source_target_pairs={{0,2},{2,4},{4,6},{6,8},{8,10},{10,12},{12,14},{14,0},{1,3},{3,5},... | collective-permute-start | bytes 3145736 | tf_op jit(solution)/shard_map/ppermute | solution.py:14
  26.9 3.0 %collective-permute-start.1 = (bf16[4,8,128,128]{3,2,1,0:T(8,128)(2,1)S(1)}, bf16[4,8,128,128]{3,2,1,0:T(8,128)(2,1)}, u32[]{:S(2)}, u32[]{:S(2)}) collective-permute-start(bf16[4,8,128,128]{3,2,1,0:T(8,128)(2,1)S(1)} %get-tuple-element.31), channel_id=1, source_target_pairs={{0,14},{2,0},{4,2},{6,4},{8,6},{10,8},{12,10},{14,12},{1,15},{3,1}... | collective-permute-start | bytes 3145736 | tf_op jit(solution)/shard_map/ppermute | solution.py:14
  29.8 0.0 copy-done.1
  29.8 0.1 broadcast_compare_fusion
  29.9 0.1 reshape.50
  30.0 0.0 collective-permute-done.2
  30.0 0.0 collective-permute-done.3
  30.1 0.6 gather_fusion
  30.7 0.7 fusion.14
  31.4 0.7 select_reduce_fusion
  32.1 0.1 copy.9
  32.3 0.1 reshape.58
  32.4 40.1 %collective-permute-done = bf16[4,8,128,128]{3,2,1,0:T(8,128)(2,1)} collective-permute-done((bf16[4,8,128,128]{3,2,1,0:T(8,128)(2,1)}, bf16[4,8,128,128]{3,2,1,0:T(8,128)(2,1)}, u32[]{:S(2)}, u32[]{:S(2)}) %collective-permute-start) | collective-permute-done | bytes 1048608 | tf_op jit(solution)/shard_map/ppermute | solution.py:14
  72.5 2.0 %collective-permute-done.1 = bf16[4,8,128,128]{3,2,1,0:T(8,128)(2,1)} collective-permute-done((bf16[4,8,128,128]{3,2,1,0:T(8,128)(2,1)S(1)}, bf16[4,8,128,128]{3,2,1,0:T(8,128)(2,1)}, u32[]{:S(2)}, u32[]{:S(2)}) %collective-permute-start.1) | collective-permute-done | bytes 1048608 | tf_op jit(solution)/shard_map/ppermute | solution.py:14
  74.5 0.0 copy-done
  74.5 1.8 %pad_maximum_fusion = bf16[16,8,128,128]{3,2,1,0:T(8,128)(2,1)S(1)} fusion(bf16[4,8,128,128]{3,2,1,0:T(8,128)(2,1)} %collective-permute-done.1, bf16[8,8,128,128]{3,2,1,0:T(8,128)(2,1)S(1)} %copy-done, bf16[4,8,128,128]{3,2,1,0:T(8,128)(2,1)} %collective-permute-done), kind=kLoop, calls=%fused_computation.2 | loop fusion | flops 4194304 | bytes 8388608 | tf_op jit(solution)/shard_map/concatenate | solution.py:31
  76.3 2.8 %concatenate.10 = bf16[129,128,128]{2,1,0:T(8,128)(2,1)} pad(bf16[128,128,128]{2,1,0:T(8,128)(2,1)S(1)} %bitcast.63, bf16[]{:T(256)} %constant.26.clone.1), padding=0_1x0_0x0_0 | pad | bytes 8421378 | tf_op jit(solution)/shard_map/concatenate | solution.py:36
  79.1 10.7 %gather_fusion.1 = bf16[256,128,128]{2,1,0:T(8,128)(2,1)} fusion(bf16[129,128,128]{2,1,0:T(8,128)(2,1)} %concatenate.10, s32[1024]{0:T(1024)S(1)} %pad_clamp_fusion), kind=kCustom, calls=%fused_computation.1 | custom fusion | bytes 16778240 | tf_op jit(solution)/shard_map/while/body/eval_jaxpr/gather | solution.py:51
  89.8 7.1 %fusion.11 = bf16[8,4,128,128]{2,3,1,0:T(8,128)(2,1)} fusion(bf16[8,8,4,128,128]{4,3,2,1,0:T(8,128)(2,1)} %bitcast.64, bf16[8,8,128,128]{3,2,1,0:T(8,128)(2,1)S(1)} %copy-done), kind=kOutput, calls=%fused_computation.12 | convolution fusion | flops 1074266112 | bytes 11534336 | tf_op jit(solution)/shard_map/while/body/eval_jaxpr/ijab,ijsbc->isac/dot_general | solution.py:52
  96.8 0.0 all-gather.5.cloned.1.call-update
  96.9 10.7 %all-gather.5.cloned.1.call-done = bf16[8,8,128,128]{2,3,1,0:T(8,128)(2,1)} async-done(((bf16[8,4,128,128]{2,3,1,0:T(8,128)(2,1)}), bf16[8,8,128,128]{2,3,1,0:T(8,128)(2,1)}) %all-gather.5.cloned.1.call-update) | async-done | bytes 2097168 | tf_op jit(solution)/shard_map/all_gather | solution.py:79
  107.6 7.0 %fusion.2 = bf16[8,4,128,128]{2,3,1,0:T(8,128)(2,1)S(1)} fusion(bf16[8,4,128,128]{2,3,1,0:T(8,128)(2,1)} %fusion.11, bf16[8,8,4,128,128]{4,3,2,1,0:T(8,128)(2,1)} %bitcast.65, bf16[8,8,128,128]{2,3,1,0:T(8,128)(2,1)} %all-gather.5.cloned.1.call-done), kind=kOutput, calls=%fused_computation.6 | convolution fusion | flops 1076363264 | bytes 12582912 | tf_op jit(solution)/shard_map/while/body/eval_jaxpr/ijab,ijsbc->isac/dot_general | solution.py:52
  114.6 1.3 %copy.13 = bf16[8,4,128,128]{3,2,1,0:T(8,128)(2,1)} copy(bf16[8,4,128,128]{2,3,1,0:T(8,128)(2,1)S(1)} %fusion.2) | data formatting | bytes 2097152 | tf_op jit(solution)/shard_map/convert_element_type | solution.py:81
  (7 shorter events, 0.0 us)
Async XLA Ops:
  6.5 23.3 %copy-start.1 = (s32[8,8]{1,0:T(8,128)S(1)}, s32[8,8]{1,0:T(8,128)}, u32[]{:S(2)}) copy-start(s32[8,8]{1,0:T(8,128)} %param.3) | copy-start | bytes 772
  6.5 15.7 %all-gather.3.cloned.1.call-start = ((), (), s32[]{:S(2)}) async-start(), calls=%async_computation | async-start | bytes 3145728 | tf_op jit(solution)/shard_map/all_gather | solution.py:26
  7.3 100.3 %all-gather.5.cloned.1.call-start = ((), (), s32[]{:S(2)}) async-start(), calls=%async_computation.1 | async-start | bytes 3145728 | tf_op jit(solution)/shard_map/all_gather | solution.py:79
  8.1 21.9 %collective-permute-start.2 = (s32[4,8]{1,0:T(4,128)S(1)}, s32[4,8]{1,0:T(4,128)S(1)}, u32[]{:S(2)}, u32[]{:S(2)}) collective-permute-start(s32[4,8]{1,0:T(4,128)S(1)} %get-tuple-element.34), channel_id=1, source_target_pairs={{0,2},{2,4},{4,6},{6,8},{8,10},{10,12},{12,14},{14,0},{1,3},{3,5},... | collective-permute-start | bytes 392 | tf_op jit(solution)/shard_map/ppermute | solution.py:14
  11.1 19.0 %collective-permute-start.3 = (s32[4,8]{1,0:T(4,128)S(1)}, s32[4,8]{1,0:T(4,128)S(1)}, u32[]{:S(2)}, u32[]{:S(2)}) collective-permute-start(s32[4,8]{1,0:T(4,128)S(1)} %get-tuple-element.40), channel_id=1, source_target_pairs={{0,14},{2,0},{4,2},{6,4},{8,6},{10,8},{12,10},{14,12},{1,15},{3,1}... | collective-permute-start | bytes 392 | tf_op jit(solution)/shard_map/ppermute | solution.py:14
  22.2 52.3 %copy-start = (bf16[8,8,128,128]{3,2,1,0:T(8,128)(2,1)S(1)}, bf16[8,8,128,128]{3,2,1,0:T(8,128)(2,1)}, u32[]{:S(2)}) copy-start(bf16[8,8,128,128]{3,2,1,0:T(8,128)(2,1)} %all-gather.3.cloned.1.call-done) | copy-start | bytes 6291460
  25.1 47.4 %collective-permute-start = (bf16[4,8,128,128]{3,2,1,0:T(8,128)(2,1)}, bf16[4,8,128,128]{3,2,1,0:T(8,128)(2,1)}, u32[]{:S(2)}, u32[]{:S(2)}) collective-permute-start(bf16[4,8,128,128]{3,2,1,0:T(8,128)(2,1)} %get-tuple-element.30), channel_id=1, source_target_pairs={{0,2},{2,4},{4,6},{6,8},{8,10},{10,12},{12,14},{14,0},{1,3},{3,5},... | collective-permute-start | bytes 3145736 | tf_op jit(solution)/shard_map/ppermute | solution.py:14
  26.9 47.7 %collective-permute-start.1 = (bf16[4,8,128,128]{3,2,1,0:T(8,128)(2,1)S(1)}, bf16[4,8,128,128]{3,2,1,0:T(8,128)(2,1)}, u32[]{:S(2)}, u32[]{:S(2)}) collective-permute-start(bf16[4,8,128,128]{3,2,1,0:T(8,128)(2,1)S(1)} %get-tuple-element.31), channel_id=1, source_target_pairs={{0,14},{2,0},{4,2},{6,4},{8,6},{10,8},{12,10},{14,12},{1,15},{3,1}... | collective-permute-start | bytes 3145736 | tf_op jit(solution)/shard_map/ppermute | solution.py:14
Sparse Core Ops, SparseCore 0:
  8.9 13.2 all-gather.2
  97.0 10.5 all-gather.4
where the time goes:
time: 123 us
  waiting for transfers between devices  61 us (50%)
  local copies, waits for them, and re-layouts  19.4 us (16%)
  matrix products  14 us (11%)
  between operations  13.5 us (11%)
  starting transfers between devices  10.8 us (9%)
  other arithmetic  4.05 us (3%)
    ppermute x4, waiting for transfers between devices, from_behind(): lax.ppermute(value, axis, [(i, (i + by) % devices) for i in range(devices)])  42.1 us
    dot_general x2, matrix products, one_group(): jnp.einsum('ijab,ijsbc->isac', left_group, picked, preferred_element_type...  14 us
    ppermute x4, starting transfers between devices, from_behind(): lax.ppermute(value, axis, [(i, (i + by) % devices) for i in range(devices)])  10.8 us
    all_gather x1, waiting for transfers between devices, local(): square_whole = lax.all_gather(square, 'col', axis=1, tiled=True)  10.7 us
    gather x1, local copies, waits for them, and re-layouts, one_group(): picked = flat_blocks[index_group]  10.7 us
    all_gather x1, waiting for transfers between devices, local(): whole_rows = lax.all_gather(matrix, 'col', axis=1, tiled=True)  7.4 us
    slice x1, local copies, waits for them, and re-layouts, local(): whole_rows[local_rows - reach_rows:]  2.91 us
    concatenate x1, local copies, waits for them, and re-layouts, local(): jnp.concatenate([panel_rows.reshape(-1, block_size, block_size), jnp.zero...  2.8 us
  transfers between devices with their start and end apart: 6, of which 4 were waited for; matrix products, arithmetic and copies ran while one was open for 6% of the time, Pallas kernels for 0%

commit v1 on v0

v1 whole, which is shorter than its diff:
```python
import functools

import jax
import jax.numpy as jnp
from jax import lax
from jax.experimental import pallas as pl
from jax.experimental.pallas import tpu as pltpu
from jax.sharding import PartitionSpec as P

REACH = 4
MESH = pl.DeviceIdType.MESH


def kernel(
    rows, slots, bs,
    cols_ref, x_ref, o_ref,
    near0, near1, near2, near3, far, send0, send1, send2, send3, panel, square, result, outbox,
    local_sem, xsend_sem, xrecv_sem, hsend_sem, hrecv_sem, osend_sem, orecv_sem,
):
    half = rows // 2
    own = x_ref.shape[1]
    width = rows + REACH
    near = (near0, near1, near2, near3)
    packed = (send0, send1, send2, send3)
    q = lax.axis_index("col")
    r = lax.axis_index("row")
    devices = lax.axis_size("row")
    total = rows * devices
    sign = 1 - 2 * q
    facing = lax.rem(r + 2 * q - 1 + devices, devices)
    partner = {"col": 1 - q}
    neighbour = {"row": facing, "col": 1 - q}

    def true_row(m, core):
        return m + core * (rows - 1 - 2 * m)

    barrier = pltpu.get_barrier_semaphore()
    pl.semaphore_signal(barrier, inc=1, device_id=partner, device_id_type=MESH)
    pl.semaphore_signal(barrier, inc=1, device_id=neighbour, device_id_type=MESH)

    mine = pl.ds(q * own, own)
    loads = []
    for m in range(half):
        loads.append(
            pltpu.make_async_copy(x_ref.at[true_row(m, q)], near[m].at[mine], local_sem.at[m])
        )
    loads.append(
        pltpu.make_async_copy(
            x_ref.at[pl.ds((1 - q) * half, half)], far.at[:, mine], local_sem.at[half]
        )
    )
    for copy in loads:
        copy.start()

    offset = []
    for m in range(rows):
        i = true_row(m, q)
        row = []
        for k in range(slots):
            col = cols_ref[i, k]
            d = col - (r * rows + i)
            d = jnp.where(d > total // 2, d - total, d)
            d = jnp.where(d < -(total // 2), d + total, d)
            row.append(jnp.where(col >= 0, d * sign, 2 * total))
        offset.append(row)

    def slot_of(m, d):
        found = jnp.int32(slots)
        for k in range(slots):
            found = jnp.where(offset[m][k] == d, k, found)
        return found

    slot = [{d: slot_of(m, d) for d in range(-REACH, REACH + 1)} for m in range(rows)]

    zero = jnp.zeros((bs, bs), x_ref.dtype)
    for m in range(half):
        near[m][slots] = zero
    for f in range(rows - half):
        far[f, slots] = zero
    for m in range(half):
        result[m, width] = zero
    for j in range(width):
        m = j - REACH
        if m < 0:
            blank = range(rows + 1 + m, width)
        else:
            blank = [c for c in range(width) if not m <= c <= m + 2 * REACH]
        for c in blank:
            panel[j, :, c * bs : (c + 1) * bs] = zero

    pl.semaphore_wait(barrier, 2)

    swaps = []
    for m in range(half):
        swaps.append(
            pltpu.make_async_remote_copy(
                src_ref=x_ref.at[true_row(m, 1 - q)],
                dst_ref=near[m].at[mine],
                send_sem=xsend_sem.at[m],
                recv_sem=xrecv_sem.at[m],
                device_id=partner,
                device_id_type=MESH,
            )
        )
    swaps.append(
        pltpu.make_async_remote_copy(
            src_ref=x_ref.at[pl.ds(q * half, half)],
            dst_ref=far.at[:, mine],
            send_sem=xsend_sem.at[half],
            recv_sem=xrecv_sem.at[half],
            device_id=partner,
            device_id_type=MESH,
        )
    )
    for copy in swaps:
        copy.start()

    halos = []
    for m in range(half):
        count = rows - m
        halo = pltpu.make_async_remote_copy(
            src_ref=packed[m],
            dst_ref=panel.at[REACH - 1 - m, :, pl.ds(0, count * bs)],
            send_sem=hsend_sem.at[m],
            recv_sem=hrecv_sem.at[m],
            device_id=neighbour,
            device_id_type=MESH,
        )
        halos.append(halo)
        loads[m].wait()
        swaps[m].wait_recv()
        for n in range(count):
            d = (REACH - 1 - n) - m
            packed[m][:, n * bs : (n + 1) * bs] = near[m][slot[m][d]]
        for d in range(-REACH, REACH + 1):
            c = m + d + REACH
            panel[m + REACH, :, c * bs : (c + 1) * bs] = near[m][slot[m][d]]
        halo.start()

    loads[half].wait()
    swaps[half].wait_recv()
    for m in range(half, rows):
        f = true_row(m, q) - (1 - q) * half
        for d in range(-REACH, REACH + 1):
            c = m + d + REACH
            if c < width:
                panel[m + REACH, :, c * bs : (c + 1) * bs] = far[f, slot[m][d]]

    tile = 2 * bs

    def product(left, p, c):
        low, high = max(p, c - REACH // 2), min(p + REACH, c + REACH // 2) + 1
        a = left[:, :, low * tile : high * tile].reshape(2 * bs, (high - low) * tile)
        b = panel[2 * low : 2 * high, :, c * tile : (c + 1) * tile].reshape((high - low) * tile, tile)
        return jnp.dot(a, b, preferred_element_type=jnp.float32)

    sent = []
    for p in reversed(range(half // 2)):
        for m in ((0, 1) if p else (2, 3)):
            halos[m].wait_recv()
        first = 2 * p
        for c in range(p, p + REACH + 1):
            value = product(panel.at[first + REACH : first + REACH + 2], p, c)
            for e in range(2):
                for g in range(2):
                    m = first + e
                    d = 2 * c + g - REACH - m
                    if -REACH <= d <= REACH:
                        keep = jnp.where(slot[m][d] == slots, 0.0, 1.0).astype(jnp.float32)
                        block = value[e * bs : (e + 1) * bs, g * bs : (g + 1) * bs] * keep
                        block = block.astype(jnp.bfloat16)
                    else:
                        block = zero
                    at = (2 * c + g) * bs
                    square[m, :, at : at + bs] = block
        for c in range(p, p + REACH + 1):
            value = product(square.at[first : first + 2], p, c)
            for e in range(2):
                for g in range(2):
                    m = first + e
                    at = (2 * c + g) * bs
                    cube = value[e * bs : (e + 1) * bs, g * bs : (g + 1) * bs]
                    whole = 3.0 * square[m, :, at : at + bs].astype(jnp.float32) - 2.0 * cube
                    result[m, 2 * c + g] = whole.astype(jnp.bfloat16)
        for m in (first, first + 1):
            i = true_row(m, q)
            for core in (1 - q, q):
                for s in range(own):
                    col = cols_ref[i, core * own + s]
                    d = col - (r * rows + i)
                    d = jnp.where(d > total // 2, d - total, d)
                    d = jnp.where(d < -(total // 2), d + total, d)
                    held = (col >= 0) & (d >= -REACH) & (d <= REACH)
                    at = jnp.where(held, d * sign + (m + REACH), width)
                    if core is q:
                        o_ref[i, s] = result[m, at]
                    else:
                        outbox[m, s] = result[m, at]
            copy = pltpu.make_async_remote_copy(
                src_ref=outbox.at[m],
                dst_ref=o_ref.at[i],
                send_sem=osend_sem.at[m],
                recv_sem=orecv_sem.at[m],
                device_id=partner,
                device_id_type=MESH,
            )
            copy.start()
            sent.append((m, copy))

    for copy in swaps + halos:
        copy.wait_send()
    for m, copy in sent:
        copy.wait_send()
        pltpu.make_async_remote_copy(
            src_ref=outbox.at[m],
            dst_ref=o_ref.at[true_row(m, 1 - q)],
            send_sem=osend_sem.at[m],
            recv_sem=orecv_sem.at[m],
            device_id=partner,
            device_id_type=MESH,
        ).wait_recv()


def local(matrix, columns):
    rows, own, bs = matrix.shape[0], matrix.shape[1], matrix.shape[2]
    slots = columns.shape[1]
    half = rows // 2
    width = rows + REACH
    kind = matrix.dtype
    dma = pltpu.SemaphoreType.DMA
    return pl.pallas_call(
        functools.partial(kernel, rows, slots, bs),
        out_shape=jax.ShapeDtypeStruct(matrix.shape, kind),
        in_specs=[
            pl.BlockSpec(memory_space=pltpu.SMEM),
            pl.BlockSpec(memory_space=pl.ANY),
        ],
        out_specs=pl.BlockSpec(memory_space=pltpu.VMEM),
        scratch_shapes=[pltpu.VMEM((slots + 1, bs, bs), kind)] * half
        + [pltpu.VMEM((rows - half, slots + 1, bs, bs), kind)]
        + [pltpu.VMEM((bs, (rows - m) * bs), kind) for m in range(half)]
        + [
            pltpu.VMEM((width, bs, width * bs), kind),
            pltpu.VMEM((half, bs, width * bs), kind),
            pltpu.VMEM((half, width + 1, bs, bs), kind),
            pltpu.VMEM((half, own, bs, bs), kind),
            dma((half + 1,)),
            dma((half + 1,)),
            dma((half + 1,)),
            dma((half,)),
            dma((half,)),
            dma((half,)),
            dma((half,)),
        ],
        compiler_params=pltpu.CompilerParams(
            collective_id=0, has_side_effects=True, vmem_limit_bytes=40 * 1024 * 1024
        ),
    )(columns, matrix)


def solution(mesh):
    placed = (P(("geom", "row"), "col", None, None), P("row", None))
    return jax.shard_map(
        local,
        mesh=mesh,
        in_specs=placed,
        out_specs=P(("geom", "row"), "col", None, None),
        check_vma=False,
    )
```

time: 123 us -> 31.7 us (0.26)
  waiting for transfers between devices: 61 us -> 0 us
  Pallas kernels: 0 us -> 28.6 us
  local copies, waits for them, and re-layouts: 19.4 us -> 2.88 us
  matrix products: 14 us -> 0 us
  between operations: 13.5 us -> 0.01 us
  starting transfers between devices: 10.8 us -> 0 us
  other arithmetic: 4.05 us -> 0 us
    ppermute x4 -> x0, waiting for transfers between devices: 42.1 us -> none  [from_behind(): lax.ppermute(value, axis, [(i, (i + by) % devices) for i in range(devices)])]
    pallas_call x0 -> x1, Pallas kernels: none -> 28.6 us  [local(): pl.pallas_call(functools.partial(kernel, rows, slots, bs), out_shape=jax....]
    all_gather x2 -> x0, waiting for transfers between devices: 18.1 us -> none  [the longest x1 10.7 us: local(): square_whole = lax.all_gather(square, 'col', axis=1, tiled=True)]
    dot_general x2 -> x0, matrix products: 14 us -> none  [one_group(): jnp.einsum('ijab,ijsbc->isac', left_group, picked, preferred_element_type...]
    gather x2 -> x0, local copies, waits for them, and re-layouts: 11.3 us -> none  [the longest x1 10.7 us: one_group(): picked = flat_blocks[index_group]]
    ppermute x4 -> x0, starting transfers between devices: 10.8 us -> none  [from_behind(): lax.ppermute(value, axis, [(i, (i + by) % devices) for i in range(devices)])]
    slice x2 -> x0, local copies, waits for them, and re-layouts: 3.68 us -> none  [the longest x1 2.91 us: local(): whole_rows[local_rows - reach_rows:]]
    unnamed x4 -> x5, local copies, waits for them, and re-layouts: 0.01 us -> 2.88 us
  transfers between devices with their start and end apart: 6 -> 0, of which waited for: 4 -> 0; matrix products, arithmetic and copies ran while one was open for 6% -> 0% of each run, Pallas kernels for 0% -> 0%
where the time goes in v1:
time: 31.7 us; the launch traced here: 31.5 us
  Pallas kernels  28.6 us (90%)
  local copies, waits for them, and re-layouts  2.88 us (9%)
    pallas_call x1, Pallas kernels, local(): pl.pallas_call(functools.partial(kernel, rows, slots, bs), out_shape=jax....  28.6 us
    unnamed x5, local copies, waits for them, and re-layouts  2.88 us

profile of v1, /device:TPU:0, one launch (start us, length us, event | category | flops | bytes accessed | tf_op | source)
XLA Modules:
  0.0 31.5 jit_solution(367495063777876914)
XLA Ops:
  0.0 0.0 copy-start
  0.0 1.2 %copy-done = bf16[8,4,128,128]{3,2,1,0:T(8,128)(2,1)S(1)} copy-done((bf16[8,4,128,128]{3,2,1,0:T(8,128)(2,1)S(1)}, bf16[8,4,128,128]{3,2,1,0:T(8,128)(2,1)}, u32[]{:S(2)}) %copy-start) | copy-done | bytes 1048600
  1.2 0.0 copy-start.1
  1.2 0.7 %copy-done.1 = s32[8,8]{1,0:T(8,128)S(1)} copy-done((s32[8,8]{1,0:T(8,128)S(1)}, s32[8,8]{1,0:T(8,128)}, u32[]{:S(2)}) %copy-start.1) | copy-done | bytes 280
  1.9 28.6 %shard_map.28 = bf16[8,4,128,128]{3,2,1,0:T(8,128)(2,1)S(1)} custom-call(s32[8,8]{1,0:T(8,128)S(1)} %copy-done.1, bf16[8,4,128,128]{3,2,1,0:T(8,128)(2,1)S(1)} %copy-done), custom_call_target="tpu_custom_call" | custom-call | tf_op jit(solution)/shard_map/pallas_call | solution.py:231
  30.5 1.0 %copy.4 = bf16[8,4,128,128]{3,2,1,0:T(8,128)(2,1)} copy(bf16[8,4,128,128]{3,2,1,0:T(8,128)(2,1)S(1)} %shard_map.28) | data formatting | bytes 2097152
Async XLA Ops:
  0.0 1.2 %copy-start = (bf16[8,4,128,128]{3,2,1,0:T(8,128)(2,1)S(1)}, bf16[8,4,128,128]{3,2,1,0:T(8,128)(2,1)}, u32[]{:S(2)}) copy-start(bf16[8,4,128,128]{3,2,1,0:T(8,128)(2,1)} %x_ref.1) | copy-start | bytes 3145732
  1.2 0.7 %copy-start.1 = (s32[8,8]{1,0:T(8,128)S(1)}, s32[8,8]{1,0:T(8,128)}, u32[]{:S(2)}) copy-start(s32[8,8]{1,0:T(8,128)} %cols_ref.1) | copy-start | bytes 772

commit v2 on v1

v2 whole, which is shorter than its diff:
```python
import functools

import jax
import jax.numpy as jnp
from jax import lax
from jax.experimental import pallas as pl
from jax.experimental.pallas import tpu as pltpu
from jax.sharding import PartitionSpec as P

REACH = 4
MESH = pl.DeviceIdType.MESH


def kernel(
    rows, slots, bs,
    cols_hbm, x_ref, o_ref,
    near0, near1, near2, near3, far, send0, send1, send2, send3, panel, square, total, part, result,
    outbox, cols_ref,
    local_sem, cols_sem, xsend_sem, xrecv_sem, dsend_sem, drecv_sem, hsend_sem, hrecv_sem, osend_sem, orecv_sem,
):
    half = rows // 2
    own = x_ref.shape[1]
    width = rows + REACH
    near = (near0, near1, near2, near3)
    packed = (send0, send1, send2, send3)
    q = lax.axis_index("col")
    r = lax.axis_index("row")
    devices = lax.axis_size("row")
    count = rows * devices
    sign = 1 - 2 * q
    above = lax.rem(r + 1, devices)
    below = lax.rem(r - 1 + devices, devices)
    facing = lax.rem(r + 2 * q - 1 + devices, devices)
    partner = {"col": 1 - q}
    neighbour = {"row": facing, "col": 1 - q}

    def true_row(m, core):
        return m + core * (rows - 1 - 2 * m)

    barrier = pltpu.get_barrier_semaphore()
    pl.semaphore_signal(barrier, inc=1, device_id=neighbour, device_id_type=MESH)

    @pl.when(q == 0)
    def _():
        pl.semaphore_signal(barrier, inc=1, device_id={"row": below}, device_id_type=MESH)

    pl.semaphore_signal(barrier, inc=1, device_id=partner, device_id_type=MESH)

    table = pltpu.make_async_copy(cols_hbm, cols_ref, cols_sem)
    table.start()
    mine = pl.ds(q * own, own)
    loads = []
    for m in range(half):
        loads.append(
            pltpu.make_async_copy(x_ref.at[true_row(m, q)], near[m].at[mine], local_sem.at[m])
        )
    loads.append(
        pltpu.make_async_copy(
            x_ref.at[pl.ds((1 - q) * half, half)], far.at[:, mine], local_sem.at[half]
        )
    )
    for copy in loads:
        copy.start()

    def diagonal(m, core, to):
        at = REACH - 1 - m
        return pltpu.make_async_remote_copy(
            src_ref=x_ref.at[true_row(m, core), 0],
            dst_ref=panel.at[at, :, pl.ds(at * bs, bs)],
            send_sem=dsend_sem.at[core, m],
            recv_sem=drecv_sem.at[m],
            device_id=to,
            device_id_type=MESH,
        )

    down = [diagonal(m, 0, {"row": below, "col": 1}) for m in range(half)]
    up = [diagonal(m, 1, {"row": above, "col": 0}) for m in range(half)]

    swaps = []
    for m in range(half):
        swaps.append(
            pltpu.make_async_remote_copy(
                src_ref=x_ref.at[true_row(m, 1 - q)],
                dst_ref=near[m].at[mine],
                send_sem=xsend_sem.at[m],
                recv_sem=xrecv_sem.at[m],
                device_id=partner,
                device_id_type=MESH,
            )
        )
    swaps.append(
        pltpu.make_async_remote_copy(
            src_ref=x_ref.at[pl.ds(q * half, half)],
            dst_ref=far.at[:, mine],
            send_sem=xsend_sem.at[half],
            recv_sem=xrecv_sem.at[half],
            device_id=partner,
            device_id_type=MESH,
        )
    )

    zero = jnp.zeros((bs, bs), x_ref.dtype)
    for m in range(half):
        near[m][slots] = zero
    for f in range(rows - half):
        far[f, slots] = zero
    for m in range(half):
        result[m, width] = zero
    for j in range(width):
        m = j - REACH
        if m < 0:
            blank = range(rows + 1 + m, width)
        else:
            blank = [c for c in range(width) if not m <= c <= m + 2 * REACH]
        for c in blank:
            panel[j, :, c * bs : (c + 1) * bs] = zero

    pl.semaphore_wait(barrier, 3 - q)
    for copy in swaps[:half]:
        copy.start()

    @pl.when(q == 0)
    def _():
        for pair in zip(down, up):
            for copy in pair:
                copy.start()

    swaps[half].start()
    table.wait()

    def offset_of(i, k):
        col = cols_ref[i, k]
        d = col - (r * rows + i)
        d = jnp.where(d > count // 2, d - count, d)
        d = jnp.where(d < -(count // 2), d + count, d)
        return jnp.where(col >= 0, d * sign, 2 * count)

    offset = [[offset_of(true_row(m, q), k) for k in range(slots)] for m in range(rows)]

    def slot_of(m, d):
        found = jnp.int32(slots)
        for k in range(slots):
            found = jnp.where(offset[m][k] == d, k, found)
        return found

    slot = [{d: slot_of(m, d) for d in range(-REACH, REACH + 1)} for m in range(rows)]

    halos, pieces = [], []
    for m in range(half):
        middle, end = REACH - 1 - m, rows - m
        spans = [(middle + 1, end)] + ([(0, middle)] if middle else [])
        copies = []
        for low, high in spans:
            at = len(pieces)
            piece = pltpu.make_async_remote_copy(
                src_ref=packed[m].at[:, pl.ds(low * bs, (high - low) * bs)],
                dst_ref=panel.at[middle, :, pl.ds(low * bs, (high - low) * bs)],
                send_sem=hsend_sem.at[at],
                recv_sem=hrecv_sem.at[at],
                device_id=neighbour,
                device_id_type=MESH,
            )
            copies.append(piece)
            pieces.append(piece)
        halos.append(copies)
        loads[m].wait()
        swaps[m].wait_recv()
        for n in range(end):
            if n != middle:
                packed[m][:, n * bs : (n + 1) * bs] = near[m][slot[m][middle - n]]
        for d in range(-REACH, REACH + 1):
            c = m + d + REACH
            panel[m + REACH, :, c * bs : (c + 1) * bs] = near[m][slot[m][d]]
        for copy in copies:
            copy.start()

    loads[half].wait()
    swaps[half].wait_recv()
    for m in range(half, rows):
        f = true_row(m, q) - (1 - q) * half
        for d in range(-REACH, REACH + 1):
            c = m + d + REACH
            if c < width:
                panel[m + REACH, :, c * bs : (c + 1) * bs] = far[f, slot[m][d]]

    tile = 2 * bs

    def span(c):
        return slice(c * tile, (c + 1) * tile)

    def product(left, row, n, low, high, c):
        a = left[row : row + n, :, low * bs : high * bs].reshape(n * bs, (high - low) * bs)
        b = panel[low:high, :, span(c)].reshape((high - low) * bs, tile)
        out = jnp.dot(a, b, preferred_element_type=jnp.float32)
        return out.reshape(n, bs, tile)

    def reached(p, c):
        return 2 * max(p, c - REACH // 2), 2 * min(p + REACH, c + REACH // 2) + 2

    def finish_square(m, c):
        for g in range(2):
            at = 2 * c + g
            d = at - REACH - m
            if -REACH <= d <= REACH:
                keep = jnp.where(slot[m][d] == slots, 0.0, 1.0).astype(jnp.float32)
                block = (total[m, :, at * bs : (at + 1) * bs] * keep).astype(jnp.bfloat16)
            else:
                block = zero
            square[m, :, at * bs : (at + 1) * bs] = block

    def finish_cube(m, c, value):
        for g in range(2):
            at = 2 * c + g
            whole = 3.0 * square[m, :, at * bs : (at + 1) * bs].astype(jnp.float32)
            whole = whole - 2.0 * value[:, g * bs : (g + 1) * bs]
            result[m, at] = whole.astype(jnp.bfloat16)

    sent = []

    def hand_out(m):
        i = true_row(m, q)
        for core in (1 - q, q):
            for s in range(own):
                d = offset_of(i, core * own + s)
                at = jnp.where((d >= -REACH) & (d <= REACH), d + (m + REACH), width)
                if core is q:
                    o_ref[i, s] = result[m, at]
                else:
                    outbox[m, s] = result[m, at]
        copy = pltpu.make_async_remote_copy(
            src_ref=outbox.at[m],
            dst_ref=o_ref.at[i],
            send_sem=osend_sem.at[m],
            recv_sem=orecv_sem.at[m],
            device_id=partner,
            device_id_type=MESH,
        )
        copy.start()
        sent.append((m, copy))

    def arrive(m):
        down[m].wait_recv()
        for copy in halos[m]:
            copy.wait_recv()

    for p in range(half // 2):
        for c in range(p, p + REACH + 1):
            low, high = reached(p, c)
            total[2 * p : 2 * p + 2, :, span(c)] = product(
                panel, 2 * p + REACH, 2, max(low, REACH), high, c
            )
    arrive(0)
    arrive(1)
    for p in (1, 0):
        for c in range(p, REACH):
            total[2 * p : 2 * p + 2, :, span(c)] += product(
                panel, 2 * p + REACH, 2, REACH - 2, REACH, c
            )
        if p:
            for c in range(p, p + REACH + 1):
                finish_square(2, c)
                finish_square(3, c)
            for c in range(p, p + REACH + 1):
                low, high = reached(p, c)
                value = product(square, 2, 2, low, high, c)
                finish_cube(2, c, value[0])
                finish_cube(3, c, value[1])
            hand_out(2)
            hand_out(3)
    arrive(2)
    for c in range(3):
        total[0:2, :, span(c)] += product(panel, REACH, 2, 1, 2, c)
    for c in range(REACH + 1):
        finish_square(1, c)
    for c in range(REACH + 1):
        low, high = reached(0, c)
        finish_cube(1, c, product(square, 1, 1, max(low, 1), high, c)[0])
    hand_out(1)
    for c in (3, 4):
        finish_square(0, c)
    for c in range(1, REACH + 1):
        part[:, span(c)] = product(square, 0, 1, 6, reached(0, c)[1], c)[0]
    arrive(3)
    for c in range(3):
        total[0:1, :, span(c)] += product(panel, REACH, 1, 0, 1, c)
        finish_square(0, c)
    for c in range(REACH + 1):
        value = product(square, 0, 1, reached(0, c)[0], 6, c)[0]
        if c:
            value = value + part[:, span(c)]
        finish_cube(0, c, value)
    hand_out(0)

    for copy in swaps + pieces:
        copy.wait_send()

    @pl.when(q == 0)
    def _():
        for copy in down + up:
            copy.wait_send()

    for m, copy in sent:
        copy.wait_send()
        pltpu.make_async_remote_copy(
            src_ref=outbox.at[m],
            dst_ref=o_ref.at[true_row(m, 1 - q)],
            send_sem=osend_sem.at[m],
            recv_sem=orecv_sem.at[m],
            device_id=partner,
            device_id_type=MESH,
        ).wait_recv()


def local(matrix, columns):
    rows, own, bs = matrix.shape[0], matrix.shape[1], matrix.shape[2]
    slots = columns.shape[1]
    half = rows // 2
    assert rows == 2 * REACH and lax.axis_size("col") == 2
    width = rows + REACH
    kind = matrix.dtype
    dma = pltpu.SemaphoreType.DMA
    return pl.pallas_call(
        functools.partial(kernel, rows, slots, bs),
        out_shape=jax.ShapeDtypeStruct(matrix.shape, kind),
        in_specs=[
            pl.BlockSpec(memory_space=pltpu.HBM),
            pl.BlockSpec(memory_space=pltpu.HBM),
        ],
        out_specs=pl.BlockSpec(memory_space=pltpu.VMEM),
        scratch_shapes=[pltpu.VMEM((slots + 1, bs, bs), kind)] * half
        + [pltpu.VMEM((rows - half, slots + 1, bs, bs), kind)]
        + [pltpu.VMEM((bs, (rows - m) * bs), kind) for m in range(half)]
        + [
            pltpu.VMEM((width, bs, width * bs), kind),
            pltpu.VMEM((half, bs, width * bs), kind),
            pltpu.VMEM((half, bs, width * bs), jnp.float32),
            pltpu.VMEM((bs, width * bs), jnp.float32),
            pltpu.VMEM((half, width + 1, bs, bs), kind),
            pltpu.VMEM((half, own, bs, bs), kind),
            pltpu.SMEM(columns.shape, columns.dtype),
            dma((half + 1,)),
            dma,
            dma((half + 1,)),
            dma((half + 1,)),
            dma((2, half)),
            dma((half,)),
            dma((2 * half - 1,)),
            dma((2 * half - 1,)),
            dma((half,)),
            dma((half,)),
        ],
        compiler_params=pltpu.CompilerParams(
            collective_id=0, has_side_effects=True, vmem_limit_bytes=40 * 1024 * 1024
        ),
    )(
        pltpu.with_memory_space_constraint(columns, pltpu.HBM),
        pltpu.with_memory_space_constraint(matrix, pltpu.HBM),
    )


def solution(mesh):
    placed = (P(("geom", "row"), "col", None, None), P("row", None))
    return jax.shard_map(
        local,
        mesh=mesh,
        in_specs=placed,
        out_specs=P(("geom", "row"), "col", None, None),
        check_vma=False,
    )
```

time: 31.7 us -> 27.4 us (0.86)
  Pallas kernels: 28.6 us -> 26.3 us
  local copies, waits for them, and re-layouts: 2.88 us -> 0.97 us
    pallas_call x1, Pallas kernels: 28.6 us -> 26.3 us  [local(): pl.pallas_call(functools.partial(kernel, rows, slots, bs), out_shape=jax....]
    unnamed x5 -> x1, local copies, waits for them, and re-layouts: 2.88 us -> 0.97 us
where the time goes in v2:
time: 27.4 us; the launch traced here: 27.3 us
  Pallas kernels  26.3 us (96%)
  local copies, waits for them, and re-layouts  0.97 us (4%)
    pallas_call x1, Pallas kernels, local(): pl.pallas_call(functools.partial(kernel, rows, slots, bs), out_shape=jax....  26.3 us
    unnamed x1, local copies, waits for them, and re-layouts  0.97 us

profile of v2, /device:TPU:0, one launch (start us, length us, event | category | flops | bytes accessed | tf_op | source)
XLA Modules:
  0.0 27.3 jit_solution(1265669746827184611)
XLA Ops:
  0.0 26.3 %shard_map.28 = bf16[8,4,128,128]{3,2,1,0:T(8,128)(2,1)S(1)} custom-call(s32[8,8]{1,0:T(8,128)} %cols_hbm.1, bf16[8,4,128,128]{3,2,1,0:T(8,128)(2,1)} %x_ref.1), custom_call_target="tpu_custom_call" | custom-call | tf_op jit(solution)/shard_map/pallas_call | solution.py:322
  26.3 1.0 %copy.4 = bf16[8,4,128,128]{3,2,1,0:T(8,128)(2,1)} copy(bf16[8,4,128,128]{3,2,1,0:T(8,128)(2,1)S(1)} %shard_map.28) | data formatting | bytes 2097152

commit v3 on v2

--- a/solution.py
+++ b/solution.py
@@ -28,8 +28,6 @@
     devices = lax.axis_size("row")
     count = rows * devices
     sign = 1 - 2 * q
-    above = lax.rem(r + 1, devices)
-    below = lax.rem(r - 1 + devices, devices)
     facing = lax.rem(r + 2 * q - 1 + devices, devices)
     partner = {"col": 1 - q}
     neighbour = {"row": facing, "col": 1 - q}
@@ -39,10 +37,6 @@
 
     barrier = pltpu.get_barrier_semaphore()
     pl.semaphore_signal(barrier, inc=1, device_id=neighbour, device_id_type=MESH)
-
-    @pl.when(q == 0)
-    def _():
-        pl.semaphore_signal(barrier, inc=1, device_id={"row": below}, device_id_type=MESH)
 
     pl.semaphore_signal(barrier, inc=1, device_id=partner, device_id_type=MESH)
 
@@ -62,19 +56,19 @@
     for copy in loads:
         copy.start()
 
-    def diagonal(m, core, to):
+    def diagonal(m, source):
         at = REACH - 1 - m
         return pltpu.make_async_remote_copy(
-            src_ref=x_ref.at[true_row(m, core), 0],
+            src_ref=source,
             dst_ref=panel.at[at, :, pl.ds(at * bs, bs)],
-            send_sem=dsend_sem.at[core, m],
+            send_sem=dsend_sem.at[m],
             recv_sem=drecv_sem.at[m],
-            device_id=to,
+            device_id=neighbour,
             device_id_type=MESH,
         )
 
-    down = [diagonal(m, 0, {"row": below, "col": 1}) for m in range(half)]
-    up = [diagonal(m, 1, {"row": above, "col": 0}) for m in range(half)]
+    held = [diagonal(m, x_ref.at[true_row(m, 0), 0]) for m in range(half)]
+    passed = [diagonal(m, near[m].at[0]) for m in range(half)]
 
     swaps = []
     for m in range(half):
@@ -115,15 +109,14 @@
         for c in blank:
             panel[j, :, c * bs : (c + 1) * bs] = zero
 
-    pl.semaphore_wait(barrier, 3 - q)
+    pl.semaphore_wait(barrier, 2)
     for copy in swaps[:half]:
         copy.start()
 
     @pl.when(q == 0)
     def _():
-        for pair in zip(down, up):
-            for copy in pair:
-                copy.start()
+        for copy in held:
+            copy.start()
 
     swaps[half].start()
     table.wait()
@@ -144,6 +137,15 @@
         return found
 
     slot = [{d: slot_of(m, d) for d in range(-REACH, REACH + 1)} for m in range(rows)]
+
+    def home_of(m, k):
+        d = offset_of(true_row(m, q), k)
+        return jnp.where((d >= -REACH) & (d <= REACH), d + (m + REACH), width)
+
+    home = [
+        [[home_of(m, core * own + s) for s in range(own)] for core in (1 - q, q)]
+        for m in range(half)
+    ]
 
     halos, pieces = [], []
     for m in range(half):
@@ -165,6 +167,11 @@
         halos.append(copies)
         loads[m].wait()
         swaps[m].wait_recv()
+
+        @pl.when(q == 1)
+        def _(m=m):
+            passed[m].start()
+
         for n in range(end):
             if n != middle:
                 packed[m][:, n * bs : (n + 1) * bs] = near[m][slot[m][middle - n]]
@@ -221,12 +228,11 @@
         i = true_row(m, q)
         for core in (1 - q, q):
             for s in range(own):
-                d = offset_of(i, core * own + s)
-                at = jnp.where((d >= -REACH) & (d <= REACH), d + (m + REACH), width)
+                block = result[m, home[m][core is q][s]]
                 if core is q:
-                    o_ref[i, s] = result[m, at]
+                    o_ref[i, s] = block
                 else:
-                    outbox[m, s] = result[m, at]
+                    outbox[m, s] = block
         copy = pltpu.make_async_remote_copy(
             src_ref=outbox.at[m],
             dst_ref=o_ref.at[i],
@@ -239,7 +245,7 @@
         sent.append((m, copy))
 
     def arrive(m):
-        down[m].wait_recv()
+        held[m].wait_recv()
         for copy in halos[m]:
             copy.wait_recv()
 
@@ -291,13 +297,8 @@
         finish_cube(0, c, value)
     hand_out(0)
 
-    for copy in swaps + pieces:
+    for copy in held + swaps + pieces:
         copy.wait_send()
-
-    @pl.when(q == 0)
-    def _():
-        for copy in down + up:
-            copy.wait_send()
 
     for m, copy in sent:
         copy.wait_send()
@@ -342,7 +343,7 @@
             dma,
             dma((half + 1,)),
             dma((half + 1,)),
-            dma((2, half)),
+            dma((half,)),
             dma((half,)),
             dma((2 * half - 1,)),
             dma((2 * half - 1,)),

time: 27.4 us -> 27 us (0.985)
  Pallas kernels: 26.3 us -> 25.9 us
    pallas_call x1, Pallas kernels: 26.3 us -> 25.9 us  [local(): pl.pallas_call(functools.partial(kernel, rows, slots, bs), out_shape=jax....]
where the time goes in v3:
time: 27 us; the launch traced here: 26.9 us
  Pallas kernels  25.9 us (96%)
  local copies, waits for them, and re-layouts  0.97 us (4%)
    pallas_call x1, Pallas kernels, local(): pl.pallas_call(functools.partial(kernel, rows, slots, bs), out_shape=jax....  25.9 us
    unnamed x1, local copies, waits for them, and re-layouts  0.97 us

profile of v3, /device:TPU:0, one launch (start us, length us, event | category | flops | bytes accessed | tf_op | source)
XLA Modules:
  0.0 26.9 jit_solution(2478251396775918855)
XLA Ops:
  0.0 25.9 %shard_map.28 = bf16[8,4,128,128]{3,2,1,0:T(8,128)(2,1)S(1)} custom-call(s32[8,8]{1,0:T(8,128)} %cols_hbm.1, bf16[8,4,128,128]{3,2,1,0:T(8,128)(2,1)} %x_ref.1), custom_call_target="tpu_custom_call" | custom-call | tf_op jit(solution)/shard_map/pallas_call | solution.py:323
  25.9 1.0 %copy.4 = bf16[8,4,128,128]{3,2,1,0:T(8,128)(2,1)} copy(bf16[8,4,128,128]{3,2,1,0:T(8,128)(2,1)S(1)} %shard_map.28) | data formatting | bytes 2097152

commit v4 on v3

--- a/solution.py
+++ b/solution.py
@@ -16,7 +16,7 @@
     cols_hbm, x_ref, o_ref,
     near0, near1, near2, near3, far, send0, send1, send2, send3, panel, square, total, part, result,
     outbox, cols_ref,
-    local_sem, cols_sem, xsend_sem, xrecv_sem, dsend_sem, drecv_sem, hsend_sem, hrecv_sem, osend_sem, orecv_sem,
+    local_sem, cols_sem, xsend_sem, xrecv_sem, dsend_sem, drecv_sem, hsend_sem, hrecv_sem, osend_sem, orecv_sem, met_sem,
 ):
     half = rows // 2
     own = x_ref.shape[1]
@@ -36,7 +36,10 @@
         return m + core * (rows - 1 - 2 * m)
 
     barrier = pltpu.get_barrier_semaphore()
-    pl.semaphore_signal(barrier, inc=1, device_id=neighbour, device_id_type=MESH)
+
+    @pl.when(q == 1)
+    def _():
+        pl.semaphore_signal(barrier, inc=1, device_id=neighbour, device_id_type=MESH)
 
     pl.semaphore_signal(barrier, inc=1, device_id=partner, device_id_type=MESH)
 
@@ -109,7 +112,12 @@
         for c in blank:
             panel[j, :, c * bs : (c + 1) * bs] = zero
 
-    pl.semaphore_wait(barrier, 2)
+    pl.semaphore_wait(barrier, 2 - q)
+
+    @pl.when(q == 0)
+    def _():
+        pl.semaphore_signal(met_sem, inc=1, device_id=neighbour, device_id_type=MESH)
+
     for copy in swaps[:half]:
         copy.start()
 
@@ -170,6 +178,8 @@
 
         @pl.when(q == 1)
         def _(m=m):
+            if m == 0:
+                pl.semaphore_wait(met_sem, 1)
             passed[m].start()
 
         for n in range(end):
@@ -349,6 +359,7 @@
             dma((2 * half - 1,)),
             dma((half,)),
             dma((half,)),
+            pltpu.SemaphoreType.REGULAR,
         ],
         compiler_params=pltpu.CompilerParams(
             collective_id=0, has_side_effects=True, vmem_limit_bytes=40 * 1024 * 1024

time: 27 us -> 26.1 us (0.967)
  Pallas kernels: 25.9 us -> 24.9 us
    pallas_call x1, Pallas kernels: 25.9 us -> 24.9 us  [local(): pl.pallas_call(functools.partial(kernel, rows, slots, bs), out_shape=jax....]
where the time goes in v4:
time: 26.1 us; the launch traced here: 25.9 us
  Pallas kernels  24.9 us (95%)
  local copies, waits for them, and re-layouts  0.97 us (4%)
    pallas_call x1, Pallas kernels, local(): pl.pallas_call(functools.partial(kernel, rows, slots, bs), out_shape=jax....  24.9 us
    unnamed x1, local copies, waits for them, and re-layouts  0.97 us

profile of v4, /device:TPU:0, one launch (start us, length us, event | category | flops | bytes accessed | tf_op | source)
XLA Modules:
  0.0 25.9 jit_solution(17476241526157818438)
XLA Ops:
  0.0 24.9 %shard_map.28 = bf16[8,4,128,128]{3,2,1,0:T(8,128)(2,1)S(1)} custom-call(s32[8,8]{1,0:T(8,128)} %cols_hbm.1, bf16[8,4,128,128]{3,2,1,0:T(8,128)(2,1)} %x_ref.1), custom_call_target="tpu_custom_call" | custom-call | tf_op jit(solution)/shard_map/pallas_call | solution.py:333
  24.9 1.0 %copy.4 = bf16[8,4,128,128]{3,2,1,0:T(8,128)(2,1)} copy(bf16[8,4,128,128]{3,2,1,0:T(8,128)(2,1)S(1)} %shard_map.28) | data formatting | bytes 2097152
